TPU v7x, 32 devices: a whole 2x2x4 slice. The times are simulated.
32 devices in a mesh: groups: 2 (over x), loop: 16 (over z, y, core).
Axes of the slice: x: 2, y: 2, z: 4, core: 2. Of those that a mesh axis runs over, the one named last changes fastest.
Arguments:
- queries: bfloat16 [256, 4, 64, 128], P(('groups', 'loop')), parts along dimension 0, may hold values from -16 to 16
- new_keys: bfloat16 [256, 4, 4, 128], P(('groups', 'loop')), parts along dimension 0, may hold values from -8 to 8
- new_values: bfloat16 [256, 4, 4, 128], P(('groups', 'loop')), parts along dimension 0, may hold values from -12 to 12
- suffix_keys: bfloat16 [256, 256, 4, 128], P(('groups', 'loop')), parts along dimension 0, may hold values from -8 to 8
- suffix_values: bfloat16 [256, 256, 4, 128], P(('groups', 'loop')), parts along dimension 0, may hold values from -12 to 12
- suffix_len: int32 [256], P(('groups', 'loop')), parts along dimension 0, may hold values from 1 to 256, 16384 in all
- prefix_keys: bfloat16 [32, 64, 4, 128], P(('groups', 'loop')), parts along dimension 0, may hold values from -8 to 8
- prefix_values: bfloat16 [32, 64, 4, 128], P(('groups', 'loop')), parts along dimension 0, may hold values from -12 to 12
- block_ids: int32 [32], P(('groups', 'loop')), parts along dimension 0, may hold values from 0 to 15, each once
- block_lists: int32 [256, 4], P(('groups', 'loop')), parts along dimension 0, may hold values from 0 to 15, all different within a row
Outputs:
- attended: bfloat16 [256, 4, 64, 128], P(('groups', 'loop')), parts along dimension 0
There are 2 independent parts, one for each index of `groups`. A program takes and returns all parts, laid end to end along the dimension named above; each array names one. Nothing has to cross between parts.
Inputs may be any that keep to these rules, and one draw needn't show every extreme that they name: `block_ids`: each slot holds a different block. `block_lists`: each request names 4 different blocks; every block is named by some request. `suffix_len`: some request uses all 256 slots.
All inputs are finite; a program needn't handle non-finite values. No bound on the sum of `suffix_len` on one device may be relied on, other than what follows from the above.
Results may differ from a plain program's by a relative error of at most 0.004.
Values may be sent and summed in bfloat16 or wider, within the bound.
No kernel may reach another device: no remote copies, remote signals or barrier semaphores. Data moves between devices by JAX's collectives and lax.ppermute only.
A program may use at most 64 MiB of HBM per device.

v0:
```python
import functools
import math

import jax
import jax.numpy as jnp
from jax import lax
from jax.experimental import pallas as pl
from jax.experimental.pallas import tpu as pltpu
from jax.sharding import PartitionSpec as P


ID_ROWS = 16
NT = (((1,), (1,)), ((), ()))


def ring_of_chips(chips):
    inner = 1 << ((chips.bit_length() - 1) // 2)
    outer = chips // inner
    if inner == 1 or outer % 2:
        return list(range(chips))
    walk = [(a, 0) for a in range(outer)]
    for step, a in enumerate(reversed(range(outer))):
        row = [(a, b) for b in range(1, inner)]
        walk += row if step % 2 == 0 else row[::-1]
    return [a * inner + b for a, b in walk]


def pack_kernel(id_ref, k_hbm, v_hbm, out_ref, raw, wide, sems, *, heads, block):
    copies = [pltpu.make_async_copy(a, raw.at[i], sems.at[i]) for i, a in enumerate((k_hbm, v_hbm))]
    for c in copies:
        c.start()
    number = id_ref[0]
    high, low = number // 256, number % 256
    row = lax.broadcasted_iota(jnp.int32, (ID_ROWS, out_ref.shape[1]), 0)
    tag = jnp.where(row < ID_ROWS // 2, high, low)
    out_ref[pl.ds(2 * heads * block, ID_ROWS), :] = tag.astype(jnp.float32).astype(out_ref.dtype)
    for i in range(2):
        copies[i].wait()
        wide[i] = raw[i].astype(jnp.float32)
        for g in range(heads):
            out_ref[pl.ds((i * heads + g) * block, block), :] = wide[
                i, pl.ds(g, block, stride=heads), :
            ].astype(out_ref.dtype)


def local_kernel(len_ref, *refs, first, count, fetch, heads, steps, group, factor):
    if fetch:
        sources, refs, (lengths_ref, len_sem, sems) = refs[:5], refs[5:-3], refs[-3:]
        len_copy = pltpu.make_async_copy(len_ref, lengths_ref, len_sem)
        len_copy.start()
        len_ref = lengths_ref
        copies = [
            [
                pltpu.make_async_copy(a.at[r], b.at[r], sems.at[r, j])
                for j, (a, b) in enumerate(zip(sources, refs[:5]))
            ]
            for r in range(sources[0].shape[0])
        ]
        for c in sum(copies, []):
            c.start()
        len_copy.wait()
    q_ref, nk_ref, nv_ref, sk_ref, sv_ref, out_ref, top_ref, sum_ref, kf, vf = refs
    slots = sk_ref.shape[1] // heads
    rows = steps * group
    fresh_col = lax.broadcasted_iota(jnp.int32, (rows, steps * heads), 1)
    fresh_row = lax.broadcasted_iota(jnp.int32, (rows, steps * heads), 0)
    fresh_seen = fresh_col // heads <= fresh_row // group
    fresh_bias = [
        jnp.where(fresh_seen & (fresh_col % heads == g), 0.0, -jnp.inf) for g in range(heads)
    ]
    slot = lax.broadcasted_iota(jnp.int32, (1, slots), 1)
    for i in range(count):
        r = first + i
        if fetch:
            for c in copies[r]:
                c.wait()
        kf[i % 2] = sk_ref[r].astype(jnp.float32)
        vf[i % 2] = sv_ref[r].astype(jnp.float32)
        bias = jnp.where(slot < len_ref[r], 0.0, -jnp.inf)
        fresh_k, fresh_v = nk_ref[r], nv_ref[r]
        scores, fresh, values = [], [], []
        for g in range(heads):
            q = jnp.concatenate(
                [q_ref[r, s, g * group : (g + 1) * group, :] for s in range(steps)], axis=0
            )
            k = kf[i % 2, pl.ds(g, slots, stride=heads), :].astype(jnp.bfloat16)
            values.append(vf[i % 2, pl.ds(g, slots, stride=heads), :].astype(jnp.bfloat16))
            scores.append(lax.dot_general(q, k, NT, preferred_element_type=jnp.float32) + bias)
            fresh.append(
                lax.dot_general(q, fresh_k, NT, preferred_element_type=jnp.float32) + fresh_bias[g]
            )
        for g in range(heads):
            top = jnp.maximum(
                jnp.max(scores[g], axis=1, keepdims=True), jnp.max(fresh[g], axis=1, keepdims=True)
            )
            w = jnp.exp2((scores[g] - top) * factor)
            wf = jnp.exp2((fresh[g] - top) * factor)
            total = jnp.sum(w, axis=1, keepdims=True) + jnp.sum(wf, axis=1, keepdims=True)
            out_ref[i, g] = jnp.dot(
                w.astype(jnp.bfloat16), values[g], preferred_element_type=jnp.float32
            ) + jnp.dot(wf.astype(jnp.bfloat16), fresh_v, preferred_element_type=jnp.float32)
            top_ref[i, g] = jnp.broadcast_to(top, top_ref.shape[2:])
            sum_ref[i, g] = jnp.broadcast_to(total, sum_ref.shape[2:])
    if fetch:
        for c in sum(copies[first + count :], []):
            c.wait()


def prior_kernel(
    list_ref, q_ref, *refs, blocks, layout, spans, heads, block, named, steps, group, factor,
):
    pieces = len(spans)
    parts, loads = refs[: 3 * pieces], refs[3 * pieces : 3 * pieces + len(layout)]
    out_hbm, kv, out_ref, slot_of, sems, gather_sem = refs[3 * pieces + len(layout) :]
    home = [(parts[3 * p : 3 * p + 3], i) for p, (_, count) in enumerate(spans) for i in range(count)]
    requests, lanes = q_ref.shape[0], q_ref.shape[3]
    half = ID_ROWS // 2
    outs = [pltpu.make_async_copy(out_ref.at[r], out_hbm.at[r], sems.at[r]) for r in range(requests)]
    for ref, place in zip(loads, layout):
        if place is None:
            whole = pltpu.make_async_copy(ref, kv, gather_sem)
            whole.start()
            whole.wait()
        else:
            kv[place[0], pl.ds(place[1], ref.shape[0]), :] = ref[...]
    for p in range(blocks):
        tag = kv[p, pl.ds(2 * heads * block, ID_ROWS), :].astype(jnp.float32)
        slot_of[jnp.max(tag[:half] * 256.0 + tag[half:]).astype(jnp.int32)] = p
    for r in range(requests):
        places = [slot_of[list_ref[j, r]] for j in range(named)]
        (near_out, near_top, near_sum), i = home[r]
        scores, values = [], []
        for g in range(heads):
            q = jnp.concatenate(
                [q_ref[r, s, g * group : (g + 1) * group, :] for s in range(steps)], axis=0
            )
            k = jnp.concatenate([kv[p, pl.ds(g * block, block), :] for p in places], axis=0)
            values.append(
                jnp.concatenate([kv[p, pl.ds((heads + g) * block, block), :] for p in places], axis=0)
            )
            scores.append(lax.dot_general(q, k, NT, preferred_element_type=jnp.float32))
        for g in range(heads):
            near = near_top[i, g]
            best = jnp.max(scores[g], axis=1, keepdims=True)
            top = jnp.maximum(near, jnp.broadcast_to(best, near.shape))
            w = [
                jnp.exp2((scores[g][:, c : c + lanes] - top) * factor)
                for c in range(0, named * block, lanes)
            ]
            keep = jnp.exp2((near - top) * factor)
            total = near_sum[i, g] * keep + jnp.sum(sum(w[1:], w[0]), axis=1, keepdims=True)
            weights = jnp.concatenate([x.astype(jnp.bfloat16) for x in w], axis=1)
            mixed = near_out[i, g] * keep + jnp.dot(
                weights, values[g], preferred_element_type=jnp.float32
            )
            mixed = (mixed / total).astype(out_ref.dtype)
            for s in range(steps):
                out_ref[r, s, g * group : (g + 1) * group, :] = mixed[s * group : (s + 1) * group]
        outs[r].start()
    for c in outs:
        c.wait()


def partial_kernel(
    list_ref, q_ref, *refs, have, spans, collect, heads, block, named, steps, group, factor,
):
    pieces = len(spans)
    parts, refs = refs[: 3 * pieces], refs[3 * pieces :]
    home = [(parts[3 * p : 3 * p + 3], i) for p, (_, count) in enumerate(spans) for i in range(count)]
    if collect:
        loads, (kv, out_ref, top_ref, sum_ref, slot_of) = refs[:have], refs[have:]
        for p in range(have):
            kv[p] = loads[p][...]
    else:
        kv, out_ref, top_ref, sum_ref, slot_of = refs
    lanes = q_ref.shape[3]
    half = ID_ROWS // 2
    for p in range(slot_of.shape[0]):
        slot_of[p] = -1
    for p in range(have):
        tag = kv[p, pl.ds(2 * heads * block, ID_ROWS), :].astype(jnp.float32)
        slot_of[jnp.max(tag[:half] * 256.0 + tag[half:]).astype(jnp.int32)] = p
    which = lax.broadcasted_iota(jnp.int32, (1, named * block), 1) // block
    for o, ((near_out, near_top, near_sum), i) in enumerate(home):
        r = spans[0][0] + o
        spots = [slot_of[list_ref[j, r]] for j in range(named)]
        places = [jnp.maximum(x, 0) for x in spots]
        bias = jnp.zeros(which.shape, jnp.float32)
        for j in range(named):
            bias = jnp.where(which == j, jnp.where(spots[j] < 0, -jnp.inf, 0.0), bias)
        scores, values = [], []
        for g in range(heads):
            q = jnp.concatenate(
                [q_ref[r, s, g * group : (g + 1) * group, :] for s in range(steps)], axis=0
            )
            k = jnp.concatenate([kv[p, pl.ds(g * block, block), :] for p in places], axis=0)
            values.append(
                jnp.concatenate([kv[p, pl.ds((heads + g) * block, block), :] for p in places], axis=0)
            )
            scores.append(lax.dot_general(q, k, NT, preferred_element_type=jnp.float32) + bias)
        for g in range(heads):
            near = near_top[i, g]
            best = jnp.max(scores[g], axis=1, keepdims=True)
            top = jnp.maximum(near, jnp.broadcast_to(best, near.shape))
            w = [
                jnp.exp2((scores[g][:, c : c + lanes] - top) * factor)
                for c in range(0, named * block, lanes)
            ]
            keep = jnp.exp2((near - top) * factor)
            sum_ref[o, g] = near_sum[i, g] * keep + jnp.sum(sum(w[1:], w[0]), axis=1, keepdims=True)
            weights = jnp.concatenate([x.astype(jnp.bfloat16) for x in w], axis=1)
            out_ref[o, g] = near_out[i, g] * keep + jnp.dot(
                weights, values[g], preferred_element_type=jnp.float32
            )
            top_ref[o, g] = top


def final_kernel(list_ref, q_ref, *refs, spans, batch, heads, block, named, steps, group, factor):
    pieces = len(spans)
    parts, (one_ref, two_ref, out_hbm, out_ref, sems) = refs[: 3 * pieces], refs[3 * pieces :]
    home = [(parts[3 * p : 3 * p + 3], i) for p, (_, count) in enumerate(spans) for i in range(count)]
    half, rows = ID_ROWS // 2, steps * group
    loads = (one_ref, two_ref)
    numbers = []
    for load in loads:
        tag = load[pl.ds(2 * heads * block, ID_ROWS), :].astype(jnp.float32)
        numbers.append(jnp.max(tag[:half] * 256.0 + tag[half:]).astype(jnp.int32))
    which = lax.broadcasted_iota(jnp.int32, (1, 2 * block), 1) // block
    outs = []
    for start in range(0, len(home), batch):
        span = range(start, min(start + batch, len(home)))
        biases = []
        for r in span:
            bias = jnp.full(which.shape, -jnp.inf, jnp.float32)
            for b in range(2):
                asked = list_ref[0, r] == numbers[b]
                for j in range(1, named):
                    asked = jnp.logical_or(asked, list_ref[j, r] == numbers[b])
                bias = jnp.where(which == b, jnp.where(asked, 0.0, -jnp.inf), bias)
            biases.append(bias)
        for g in range(heads):
            k = jnp.concatenate([x[pl.ds(g * block, block), :] for x in loads], axis=0)
            v = jnp.concatenate([x[pl.ds((heads + g) * block, block), :] for x in loads], axis=0)
            q = jnp.concatenate(
                [q_ref[r, s, g * group : (g + 1) * group, :] for r in span for s in range(steps)], axis=0
            )
            scores = lax.dot_general(q, k, NT, preferred_element_type=jnp.float32)
            weights, keeps, totals = [], [], []
            for o, r in enumerate(span):
                (_, near_top, near_sum), i = home[r]
                near = near_top[i, g]
                own = scores[o * rows : (o + 1) * rows] + biases[o]
                best = jnp.max(own, axis=1, keepdims=True)
                top = jnp.maximum(near, jnp.broadcast_to(best, near.shape))
                w = jnp.exp2((own - top[:, :1] if top.shape[1] != own.shape[1] else own - top) * factor)
                keep = jnp.exp2((near - top) * factor)
                totals.append(near_sum[i, g] * keep + jnp.sum(w, axis=1, keepdims=True))
                weights.append(w.astype(jnp.bfloat16))
                keeps.append(keep)
            mixed = jnp.dot(jnp.concatenate(weights, axis=0), v, preferred_element_type=jnp.float32)
            for o, r in enumerate(span):
                (near_out, _, _), i = home[r]
                out = near_out[i, g] * keeps[o] + mixed[o * rows : (o + 1) * rows]
                out = (out / totals[o]).astype(out_ref.dtype)
                for s in range(steps):
                    out_ref[r, s, g * group : (g + 1) * group, :] = out[s * group : (s + 1) * group]
        for r in span:
            outs.append(pltpu.make_async_copy(out_ref.at[r], out_hbm.at[r], sems.at[r]))
            outs[-1].start()
    for c in outs:
        c.wait()


def per_device(
    queries, new_keys, new_values, suffix_keys, suffix_values, suffix_len,
    prefix_keys, prefix_values, block_ids, block_lists, *, devices, pieces=3,
):
    requests, steps, head_count, width = queries.shape
    heads = new_keys.shape[2]
    group = head_count // heads
    slots = suffix_keys.shape[1]
    block = prefix_keys.shape[1]
    named = block_lists.shape[1]
    factor = math.log2(math.e) / math.sqrt(width)
    rows = steps * group
    kind = queries.dtype
    far = pl.BlockSpec(memory_space=pltpu.HBM)
    vmem = pl.BlockSpec(memory_space=pltpu.VMEM)
    smem = pl.BlockSpec(memory_space=pltpu.SMEM)
    load_rows = 2 * heads * block + ID_ROWS
    tie = lambda *arrays: lax.optimization_barrier(arrays)
    away = functools.partial(pltpu.with_memory_space_constraint, memory_space=pltpu.HBM)
    near = functools.partial(pltpu.with_memory_space_constraint, memory_space=pltpu.VMEM)
    limit = lambda mib: pltpu.CompilerParams(vmem_limit_bytes=mib << 20)

    load = pl.pallas_call(
        functools.partial(pack_kernel, heads=heads, block=block),
        out_shape=pltpu.VMEM((load_rows, width), kind),
        in_specs=[smem, far, far],
        out_specs=vmem,
        scratch_shapes=[
            pltpu.VMEM((2, heads * block, width), kind),
            pltpu.VMEM((2, heads * block, width), jnp.float32),
            pltpu.SemaphoreType.DMA((2,)),
        ],
        compiler_params=limit(4),
        name="pack",
    )(
        block_ids,
        away(prefix_keys.reshape(heads * block, width)),
        away(prefix_values.reshape(heads * block, width)),
    )

    flat = [
        queries,
        new_keys.reshape(requests, steps * heads, width),
        new_values.reshape(requests, steps * heads, width),
        suffix_keys.reshape(requests, slots * heads, width),
        suffix_values.reshape(requests, slots * heads, width),
    ]
    sizes = [(requests + p) // pieces for p in range(pieces)][::-1]
    spans = [(sum(sizes[:p]), sizes[p]) for p in range(pieces)]

    def local(piece, lengths, arrays):
        first, count = spans[piece]
        fetch = piece == 0
        stats = [pltpu.VMEM((count, heads, rows, width), jnp.float32)] * 3
        handed = [pltpu.VMEM(x.shape, x.dtype) for x in arrays] if fetch else []
        return pl.pallas_call(
            functools.partial(
                local_kernel, first=first, count=count, fetch=fetch, heads=heads, steps=steps,
                group=group, factor=factor,
            ),
            out_shape=handed + stats,
            in_specs=[far] * 6 if fetch else [smem] + [vmem] * 5,
            out_specs=[vmem] * len(handed + stats),
            scratch_shapes=[pltpu.VMEM((2, slots * heads, width), jnp.float32)] * 2
            + [
                pltpu.SMEM((requests,), jnp.int32),
                pltpu.SemaphoreType.DMA,
                pltpu.SemaphoreType.DMA((requests, 5)),
            ][: 3 * fetch],
            compiler_params=limit(8),
        )(away(lengths) if fetch else lengths, *[(away if fetch else near)(x) for x in arrays])

    chips = devices // 2
    rounds = chips // 2
    if 2 <= chips <= 16 and chips % 2 == 0:
        ring = ring_of_chips(chips)
        ahead = [(2 * a + c, 2 * b + c) for a, b in zip(ring, ring[1:] + ring[:1]) for c in range(2)]
        back = [(b, a) for a, b in ahead]
        swap = [(d, d ^ 1) for d in range(devices)]
        send = lambda x, pairs: lax.ppermute(x, "loop", pairs)
        right = left = load
        loads, layout, held, parts, fresh = [load], [(0, 0)], [], [], []
        waiting = [load]

        for step in range(rounds):
            if step == 0:
                right, *flat = tie(load, *flat)
                left, lengths = right, suffix_len
            else:
                right, *fresh = tie(right, *fresh)
                lengths, left = tie(suffix_len, left)
                if step == 1:
                    held, fresh = fresh[:5], fresh[5:]
                parts += fresh
                fresh = []
            last = step == rounds - 1
            ahead_of = send(right, ahead)
            back_of = left if last else send(left, back)
            if step < pieces:
                fresh = local(step, lengths, held or flat)
            if last:
                for x in waiting:
                    layout.append((len(layout), 0))
                    loads.append(send(x, swap))
            right, left = ahead_of, back_of
            if not last:
                for x in (right, left):
                    layout.append((len(layout), 0))
                    loads.append(x)
                    waiting.append(x)
        if rounds == 1:
            held, fresh = fresh[:5], fresh[5:]
        parts += fresh
        lists = block_lists.T
        for piece in range(min(rounds, pieces), pieces):
            parts += local(piece, suffix_len, held)
        sizes = dict(heads=heads, block=block, named=named, steps=steps, group=group, factor=factor)

        def partial(spans, parts, lists, sources, collect):
            count = sum(n for _, n in spans)
            have = devices - 2
            stats = [pltpu.VMEM((count, heads, rows, width), jnp.float32)] * 3
            made = [pltpu.VMEM((have, load_rows, width), kind)] if collect else []
            return pl.pallas_call(
                functools.partial(partial_kernel, have=have, spans=spans, collect=collect, **sizes),
                out_shape=made + stats,
                in_specs=[smem] + [vmem] * (1 + len(parts) + len(sources)),
                out_specs=[vmem] * len(made + stats),
                scratch_shapes=[pltpu.SMEM((devices,), jnp.int32)],
                compiler_params=limit(4),
            )(lists, *[near(x) for x in (held[0], *parts, *sources)])

        collected, *early = partial(spans[:1], parts[:3], lists, loads, True)
        right, *early = tie(right, *early)
        lists, right = tie(lists, right)
        other = send(right, swap)
        late = partial(spans[1:], parts[3:], lists, [collected], False)
        groups = [spans[0], (spans[1][0], requests - spans[1][0])]
        return pl.pallas_call(
            functools.partial(final_kernel, spans=groups, batch=-(-requests // 2), **sizes),
            out_shape=jax.ShapeDtypeStruct(queries.shape, kind),
            in_specs=[smem] + [vmem] * 9,
            out_specs=far,
            scratch_shapes=[pltpu.VMEM(queries.shape, kind), pltpu.SemaphoreType.DMA((requests,))],
            compiler_params=limit(8),
            name="final",
        )(lists, *[near(x) for x in (held[0], *early, *late, right, other)])
    gathered = lax.all_gather(load, "loop", axis=0)
    *held, a, b, c = local(0, suffix_len, flat)
    parts = [a, b, c]
    loads, layout = [away(gathered)], [None]
    for piece in range(1, pieces):
        parts += local(piece, suffix_len, held)

    return pl.pallas_call(
        functools.partial(
            prior_kernel, blocks=devices, layout=layout, spans=spans, heads=heads, block=block, named=named,
            steps=steps, group=group, factor=factor,
        ),
        out_shape=jax.ShapeDtypeStruct(queries.shape, kind),
        in_specs=[smem] + [vmem] * (1 + 3 * pieces) + [far if x is None else vmem for x in layout],
        out_specs=far,
        scratch_shapes=[
            pltpu.VMEM((devices, load_rows, width), kind),
            pltpu.VMEM(queries.shape, kind),
            pltpu.SMEM((devices,), jnp.int32),
            pltpu.SemaphoreType.DMA((requests,)),
            pltpu.SemaphoreType.DMA,
        ],
        compiler_params=limit(24),
        name="prior",
    )(block_lists.T, near(held[0]), *[near(x) for x in parts], *loads)


def solution(mesh):
    split = ("groups", "loop")
    in_specs = tuple(
        P(split, *([None] * (rank - 1))) for rank in (4, 4, 4, 4, 4, 1, 4, 4, 1, 2)
    )

    def body(*arrays):
        return per_device(*arrays, devices=mesh.shape["loop"])

    return jax.shard_map(
        body, mesh=mesh, in_specs=in_specs, out_specs=P(split, None, None, None), check_vma=False
    )
```

profile of v0, /device:TPU:0, one launch (start us, length us, event | category | flops | bytes accessed | tf_op | source)
XLA Modules:
  0.0 30.9 jit_solution(16981239585251051012)
XLA Ops:
  0.7 0.9 %pack.1.refs_3_ = bf16[528,128]{1,0:T(8,128)(2,1)S(1)} custom-call(s32[1]{0:T(128)S(6)} %copy.11.id_ref, bf16[256,128]{1,0:T(8,128)(2,1)} %bitcast.12, bf16[256,128]{1,0:T(8,128)(2,1)} %bitcast.13), custom_call_target="tpu_custom_call" | custom-call | tf_op jit(solution)/shard_map/pack/pallas_call | solution.py:296
  1.6 0.0 copy-start.1
  1.6 3.1 %collective-permute-start = (bf16[528,128]{1,0:T(8,128)(2,1)S(1)}, bf16[528,128]{1,0:T(8,128)(2,1)S(1)}, u32[]{:S(2)}, u32[]{:S(2)}) collective-permute-start(bf16[528,128]{1,0:T(8,128)(2,1)S(1)} %pack.1.refs_3_), channel_id=1, source_target_pairs={{0,4},{1,5},{4,8},{5,9},{8,12},{9,13},{12,14},{13,15},{14,10},{15,... | collective-permute-start | bytes 405512 | tf_op jit(solution)/shard_map/ppermute | solution.py:353
  4.7 0.0 collective-permute-start.2
  4.7 3.1 %shard_map.100 = (bf16[8,4,64,128]{3,2,1,0:T(8,128)(2,1)S(1)}, bf16[8,16,128]{2,1,0:T(8,128)(2,1)S(1)}, bf16[8,16,128]{2,1,0:T(8,128)(2,1)S(1)}, bf16[8,1024,128...) custom-call(s32[8]{0:T(128)} %len_ref.3, ...), custom_call_target="tpu_custom_call" | custom-call | tf_op jit(solution)/shard_map/pallas_call | solution.py:329
  7.8 0.5 %collective-permute-done.refs_4_ = bf16[528,128]{1,0:T(8,128)(2,1)S(1)} collective-permute-done((bf16[528,128]{1,0:T(8,128)(2,1)S(1)}, bf16[528,128]{1,0:T(8,128)(2,1)S(1)}, u32[]{:S(2)}, u32[]{:S(2)}) %collective-permute-start) | collective-permute-done | bytes 135200 | tf_op jit(solution)/shard_map/ppermute | solution.py:353
  8.2 1.8 %collective-permute-start.1 = (bf16[528,128]{1,0:T(8,128)(2,1)S(1)}, bf16[528,128]{1,0:T(8,128)(2,1)S(1)}, u32[]{:S(2)}, u32[]{:S(2)}) collective-permute-start(bf16[528,128]{1,0:T(8,128)(2,1)S(1)} %collective-permute-done.refs_4_), channel_id=1, source_target_pairs={{0,4},{1,5},{4,8},{5,9},{8,12},{9,13},{12,14},{13,15},{14,10},{15,... | collective-permute-start | bytes 405512 | tf_op jit(solution)/shard_map/ppermute | solution.py:353
  10.0 0.0 collective-permute-done.2.refs_5_
  10.0 0.2 collective-permute-start.4
  10.2 0.0 collective-permute-start.7
  10.2 1.7 %shard_map.101 = (f32[3,4,64,128]{3,2,1,0:T(8,128)S(1)}, f32[3,4,64,128]{3,2,1,0:T(8,128)S(1)}, f32[3,4,64,128]{3,2,1,0:T(8,128)S(1)}) custom-call(s32[8]{0:T(128)S(1)} %copy-done.1, bf16[8,4,64,128]{3,2,1,0:T(8,128)(2,1)S(1)} %get-tuple-element.75.refs_0_.q_ref, bf16[8,16,128]{2,1,0:T(8,128)(2,1)S(1)} %get-tuple-element.76.refs_1_, ...), custom_call_target="tpu_custom_call" | custom-call | tf_op jit(solution)/shard_map/pallas_call | solution.py:329
  12.0 0.6 %collective-permute-start.8 = (bf16[528,128]{1,0:T(8,128)(2,1)S(1)}, bf16[528,128]{1,0:T(8,128)(2,1)S(1)}, u32[]{:S(2)}, u32[]{:S(2)}) collective-permute-start(bf16[528,128]{1,0:T(8,128)(2,1)S(1)} %collective-permute-done.refs_4_), channel_id=1, source_target_pairs={{0,1},{1,0},{2,3},{3,2},{4,5},{5,4},{6,7},{7,6},{8,9},{9,8},{10,11... | collective-permute-start | bytes 405512 | tf_op jit(solution)/shard_map/ppermute | solution.py:353
  12.6 0.7 %collective-permute-done.1.refs_6_ = bf16[528,128]{1,0:T(8,128)(2,1)S(1)} collective-permute-done((bf16[528,128]{1,0:T(8,128)(2,1)S(1)}, bf16[528,128]{1,0:T(8,128)(2,1)S(1)}, u32[]{:S(2)}, u32[]{:S(2)}) %collective-permute-start.1) | collective-permute-done | bytes 135200 | tf_op jit(solution)/shard_map/ppermute | solution.py:353
  13.2 1.8 %collective-permute-start.3 = (bf16[528,128]{1,0:T(8,128)(2,1)S(1)}, bf16[528,128]{1,0:T(8,128)(2,1)S(1)}, u32[]{:S(2)}, u32[]{:S(2)}) collective-permute-start(bf16[528,128]{1,0:T(8,128)(2,1)S(1)} %collective-permute-done.1.refs_6_), channel_id=1, source_target_pairs={{0,4},{1,5},{4,8},{5,9},{8,12},{9,13},{12,14},{13,15},{14,10},{15,... | collective-permute-start | bytes 405512 | tf_op jit(solution)/shard_map/ppermute | solution.py:353
  15.0 0.2 collective-permute-start.6
  15.3 1.4 %shard_map.102 = (f32[2,4,64,128]{3,2,1,0:T(8,128)S(1)}, f32[2,4,64,128]{3,2,1,0:T(8,128)S(1)}, f32[2,4,64,128]{3,2,1,0:T(8,128)S(1)}) custom-call(s32[8]{0:T(128)S(1)} %copy-done.1, bf16[8,4,64,128]{3,2,1,0:T(8,128)(2,1)S(1)} %get-tuple-element.75.refs_0_.q_ref, bf16[8,16,128]{2,1,0:T(8,128)(2,1)S(1)} %get-tuple-element.76.refs_1_, ...), custom_call_target="tpu_custom_call" | custom-call | tf_op jit(solution)/shard_map/pallas_call | solution.py:329
  16.7 0.0 collective-permute-done.7.refs_10_
  16.7 0.6 %collective-permute-start.10 = (bf16[528,128]{1,0:T(8,128)(2,1)S(1)}, bf16[528,128]{1,0:T(8,128)(2,1)S(1)}, u32[]{:S(2)}, u32[]{:S(2)}) collective-permute-start(bf16[528,128]{1,0:T(8,128)(2,1)S(1)} %collective-permute-done.1.refs_6_), channel_id=1, source_target_pairs={{0,1},{1,0},{2,3},{3,2},{4,5},{5,4},{6,7},{7,6},{8,9},{9,8},{10,11... | collective-permute-start | bytes 405512 | tf_op jit(solution)/shard_map/ppermute | solution.py:353
  17.2 0.0 collective-permute-done.8.refs_11_
  17.2 0.1 collective-permute-start.11
  17.3 0.9 %collective-permute-done.3.refs_8_ = bf16[528,128]{1,0:T(8,128)(2,1)S(1)} collective-permute-done((bf16[528,128]{1,0:T(8,128)(2,1)S(1)}, bf16[528,128]{1,0:T(8,128)(2,1)S(1)}, u32[]{:S(2)}, u32[]{:S(2)}) %collective-permute-start.3) | collective-permute-done | bytes 135200 | tf_op jit(solution)/shard_map/ppermute | solution.py:353
  18.2 1.8 %collective-permute-done.6.refs_9_ = bf16[528,128]{1,0:T(8,128)(2,1)S(1)} collective-permute-done((bf16[528,128]{1,0:T(8,128)(2,1)S(1)}, bf16[528,128]{1,0:T(8,128)(2,1)S(1)}, u32[]{:S(2)}, u32[]{:S(2)}) %collective-permute-start.6) | collective-permute-done | bytes 135200 | tf_op jit(solution)/shard_map/ppermute | solution.py:353
  20.0 0.0 collective-permute-start.13
  20.0 0.0 collective-permute-done.9.refs_12_
  20.0 1.6 %collective-permute-start.5 = (bf16[528,128]{1,0:T(8,128)(2,1)S(1)}, bf16[528,128]{1,0:T(8,128)(2,1)S(1)}, u32[]{:S(2)}, u32[]{:S(2)}) collective-permute-start(bf16[528,128]{1,0:T(8,128)(2,1)S(1)} %collective-permute-done.3.refs_8_), channel_id=1, source_target_pairs={{0,4},{1,5},{4,8},{5,9},{8,12},{9,13},{12,14},{13,15},{14,10},{15,... | collective-permute-start | bytes 405512 | tf_op jit(solution)/shard_map/ppermute | solution.py:353
  21.6 0.0 collective-permute-done.10.refs_13_
  21.6 0.0 collective-permute-done.11.refs_14_
  21.6 0.0 collective-permute-done.12.refs_15_
  21.7 1.8 %shard_map.103 = (bf16[14,528,128]{2,1,0:T(8,128)(2,1)S(1)}, f32[3,4,64,128]{3,2,1,0:T(8,128)S(1)}, f32[3,4,64,128]{3,2,1,0:T(8,128)S(1)}, f32[3,4,64,128]{3,2,1,0:T(8,128)S(1)}) custom-call(s32[4,8]{1,0:T(4,128)S(1)} %bitcast.7, bf16[8,4,64,128]{3,2,1,0:T(8,128)(2,1)S(1)} %get-tuple-element.75.refs_0_.q_ref, ...), custom_call_target="tpu_custom_call" | custom-call | tf_op jit(solution)/shard_map/pallas_call | solution.py:397
  23.5 2.5 %collective-permute-done.5.refs_6_ = bf16[528,128]{1,0:T(8,128)(2,1)S(1)} collective-permute-done((bf16[528,128]{1,0:T(8,128)(2,1)S(1)}, bf16[528,128]{1,0:T(8,128)(2,1)S(1)}, u32[]{:S(2)}, u32[]{:S(2)}) %collective-permute-start.5) | collective-permute-done | bytes 135200 | tf_op jit(solution)/shard_map/ppermute | solution.py:353
  26.0 2.4 %shard_map.104 = (f32[5,4,64,128]{3,2,1,0:T(8,128)S(1)}, f32[5,4,64,128]{3,2,1,0:T(8,128)S(1)}, f32[5,4,64,128]{3,2,1,0:T(8,128)S(1)}) custom-call(s32[4,8]{1,0:T(4,128)S(1)} %bitcast.8, bf16[8,4,64,128]{3,2,1,0:T(8,128)(2,1)S(1)} %get-tuple-element.75.refs_0_.q_ref, f32[3,4,64,128]{3,2,1,0:T(8,128)S(1)} %get-tuple-element.102.refs_0_, ...), custom_call_target="tpu_custom_call" | custom-call | tf_op jit(solution)/shard_map/pallas_call | solution.py:397
  28.5 2.4 %final.1 = bf16[8,4,64,128]{3,2,1,0:T(8,128)(2,1)} custom-call(s32[4,8]{1,0:T(4,128)S(1)} %bitcast.9, bf16[8,4,64,128]{3,2,1,0:T(8,128)(2,1)S(1)} %get-tuple-element.75.refs_0_.q_ref, f32[3,4,64,128]{3,2,1,0:T(8,128)S(1)} %get-tuple-element.99.refs_0_, f32[3,4,64,128]{3,2,1,0:T(8,128)S(1)} %get-tuple-element.100.refs_1_, ...), custom_call_target="tpu_custom_call" | custom-call | tf_op jit(solution)/shard_map/final/pallas_call | solution.py:412
  (9 shorter events, 0.0 us)
Async XLA Ops:
  1.6 8.7 %copy-start.1 = (s32[8]{0:T(128)S(1)}, s32[8]{0:T(128)}, u32[]{:S(2)}) copy-start(s32[8]{0:T(128)} %len_ref.3) | copy-start | bytes 100
  1.6 6.6 %collective-permute-start = (bf16[528,128]{1,0:T(8,128)(2,1)S(1)}, bf16[528,128]{1,0:T(8,128)(2,1)S(1)}, u32[]{:S(2)}, u32[]{:S(2)}) collective-permute-start(bf16[528,128]{1,0:T(8,128)(2,1)S(1)} %pack.1.refs_3_), channel_id=1, source_target_pairs={{0,4},{1,5},{4,8},{5,9},{8,12},{9,13},{12,14},{13,15},{14,10},{15,... | collective-permute-start | bytes 405512 | tf_op jit(solution)/shard_map/ppermute | solution.py:353
  4.7 5.3 %collective-permute-start.2 = (bf16[528,128]{1,0:T(8,128)(2,1)S(1)}, bf16[528,128]{1,0:T(8,128)(2,1)S(1)}, u32[]{:S(2)}, u32[]{:S(2)}) collective-permute-start(bf16[528,128]{1,0:T(8,128)(2,1)S(1)} %pack.1.refs_3_), channel_id=1, source_target_pairs={{4,0},{5,1},{8,4},{9,5},{12,8},{13,9},{14,12},{15,13},{10,14},{11,... | collective-permute-start | bytes 405512 | tf_op jit(solution)/shard_map/ppermute | solution.py:353
  8.2 5.0 %collective-permute-start.1 = (bf16[528,128]{1,0:T(8,128)(2,1)S(1)}, bf16[528,128]{1,0:T(8,128)(2,1)S(1)}, u32[]{:S(2)}, u32[]{:S(2)}) collective-permute-start(bf16[528,128]{1,0:T(8,128)(2,1)S(1)} %collective-permute-done.refs_4_), channel_id=1, source_target_pairs={{0,4},{1,5},{4,8},{5,9},{8,12},{9,13},{12,14},{13,15},{14,10},{15,... | collective-permute-start | bytes 405512 | tf_op jit(solution)/shard_map/ppermute | solution.py:353
  10.0 5.0 %collective-permute-start.4 = (bf16[528,128]{1,0:T(8,128)(2,1)S(1)}, bf16[528,128]{1,0:T(8,128)(2,1)S(1)}, u32[]{:S(2)}, u32[]{:S(2)}) collective-permute-start(bf16[528,128]{1,0:T(8,128)(2,1)S(1)} %collective-permute-done.2.refs_5_), channel_id=1, source_target_pairs={{4,0},{5,1},{8,4},{9,5},{12,8},{13,9},{14,12},{15,13},{10,14},{11,... | collective-permute-start | bytes 405512 | tf_op jit(solution)/shard_map/ppermute | solution.py:353
  10.2 6.4 %collective-permute-start.7 = (bf16[528,128]{1,0:T(8,128)(2,1)S(1)}, bf16[528,128]{1,0:T(8,128)(2,1)S(1)}, u32[]{:S(2)}, u32[]{:S(2)}) collective-permute-start(bf16[528,128]{1,0:T(8,128)(2,1)S(1)} %pack.1.refs_3_), channel_id=1, source_target_pairs={{0,1},{1,0},{2,3},{3,2},{4,5},{5,4},{6,7},{7,6},{8,9},{9,8},{10,11... | collective-permute-start | bytes 405512 | tf_op jit(solution)/shard_map/ppermute | solution.py:353
  12.0 5.2 %collective-permute-start.8 = (bf16[528,128]{1,0:T(8,128)(2,1)S(1)}, bf16[528,128]{1,0:T(8,128)(2,1)S(1)}, u32[]{:S(2)}, u32[]{:S(2)}) collective-permute-start(bf16[528,128]{1,0:T(8,128)(2,1)S(1)} %collective-permute-done.refs_4_), channel_id=1, source_target_pairs={{0,1},{1,0},{2,3},{3,2},{4,5},{5,4},{6,7},{7,6},{8,9},{9,8},{10,11... | collective-permute-start | bytes 405512 | tf_op jit(solution)/shard_map/ppermute | solution.py:353
  13.2 8.4 %copy-start = (s32[8,4]{0,1:T(4,128)S(1)}, s32[8,4]{0,1:T(4,128)}, u32[]{:S(2)}) copy-start(s32[8,4]{0,1:T(4,128)} %param.19) | copy-start | bytes 388
  13.2 5.0 %collective-permute-start.3 = (bf16[528,128]{1,0:T(8,128)(2,1)S(1)}, bf16[528,128]{1,0:T(8,128)(2,1)S(1)}, u32[]{:S(2)}, u32[]{:S(2)}) collective-permute-start(bf16[528,128]{1,0:T(8,128)(2,1)S(1)} %collective-permute-done.1.refs_6_), channel_id=1, source_target_pairs={{0,4},{1,5},{4,8},{5,9},{8,12},{9,13},{12,14},{13,15},{14,10},{15,... | collective-permute-start | bytes 405512 | tf_op jit(solution)/shard_map/ppermute | solution.py:353
  15.0 5.0 %collective-permute-start.6 = (bf16[528,128]{1,0:T(8,128)(2,1)S(1)}, bf16[528,128]{1,0:T(8,128)(2,1)S(1)}, u32[]{:S(2)}, u32[]{:S(2)}) collective-permute-start(bf16[528,128]{1,0:T(8,128)(2,1)S(1)} %collective-permute-done.4.refs_7_), channel_id=1, source_target_pairs={{4,0},{5,1},{8,4},{9,5},{12,8},{13,9},{14,12},{15,13},{10,14},{11,... | collective-permute-start | bytes 405512 | tf_op jit(solution)/shard_map/ppermute | solution.py:353
  15.3 4.8 %collective-permute-start.9 = (bf16[528,128]{1,0:T(8,128)(2,1)S(1)}, bf16[528,128]{1,0:T(8,128)(2,1)S(1)}, u32[]{:S(2)}, u32[]{:S(2)}) collective-permute-start(bf16[528,128]{1,0:T(8,128)(2,1)S(1)} %collective-permute-done.2.refs_5_), channel_id=1, source_target_pairs={{0,1},{1,0},{2,3},{3,2},{4,5},{5,4},{6,7},{7,6},{8,9},{9,8},{10,11... | collective-permute-start | bytes 405512 | tf_op jit(solution)/shard_map/ppermute | solution.py:353
  16.7 5.0 %collective-permute-start.10 = (bf16[528,128]{1,0:T(8,128)(2,1)S(1)}, bf16[528,128]{1,0:T(8,128)(2,1)S(1)}, u32[]{:S(2)}, u32[]{:S(2)}) collective-permute-start(bf16[528,128]{1,0:T(8,128)(2,1)S(1)} %collective-permute-done.1.refs_6_), channel_id=1, source_target_pairs={{0,1},{1,0},{2,3},{3,2},{4,5},{5,4},{6,7},{7,6},{8,9},{9,8},{10,11... | collective-permute-start | bytes 405512 | tf_op jit(solution)/shard_map/ppermute | solution.py:353
  17.2 4.4 %collective-permute-start.11 = (bf16[528,128]{1,0:T(8,128)(2,1)S(1)}, bf16[528,128]{1,0:T(8,128)(2,1)S(1)}, u32[]{:S(2)}, u32[]{:S(2)}) collective-permute-start(bf16[528,128]{1,0:T(8,128)(2,1)S(1)} %collective-permute-done.4.refs_7_), channel_id=1, source_target_pairs={{0,1},{1,0},{2,3},{3,2},{4,5},{5,4},{6,7},{7,6},{8,9},{9,8},{10,11... | collective-permute-start | bytes 405512 | tf_op jit(solution)/shard_map/ppermute | solution.py:353
  18.2 3.4 %collective-permute-start.12 = (bf16[528,128]{1,0:T(8,128)(2,1)S(1)}, bf16[528,128]{1,0:T(8,128)(2,1)S(1)}, u32[]{:S(2)}, u32[]{:S(2)}) collective-permute-start(bf16[528,128]{1,0:T(8,128)(2,1)S(1)} %collective-permute-done.3.refs_8_), channel_id=1, source_target_pairs={{0,1},{1,0},{2,3},{3,2},{4,5},{5,4},{6,7},{7,6},{8,9},{9,8},{10,11... | collective-permute-start | bytes 405512 | tf_op jit(solution)/shard_map/ppermute | solution.py:353
  20.0 1.6 %collective-permute-start.13 = (bf16[528,128]{1,0:T(8,128)(2,1)S(1)}, bf16[528,128]{1,0:T(8,128)(2,1)S(1)}, u32[]{:S(2)}, u32[]{:S(2)}) collective-permute-start(bf16[528,128]{1,0:T(8,128)(2,1)S(1)} %collective-permute-done.6.refs_9_), channel_id=1, source_target_pairs={{0,1},{1,0},{2,3},{3,2},{4,5},{5,4},{6,7},{7,6},{8,9},{9,8},{10,11... | collective-permute-start | bytes 405512 | tf_op jit(solution)/shard_map/ppermute | solution.py:353
  20.0 6.0 %collective-permute-start.5 = (bf16[528,128]{1,0:T(8,128)(2,1)S(1)}, bf16[528,128]{1,0:T(8,128)(2,1)S(1)}, u32[]{:S(2)}, u32[]{:S(2)}) collective-permute-start(bf16[528,128]{1,0:T(8,128)(2,1)S(1)} %collective-permute-done.3.refs_8_), channel_id=1, source_target_pairs={{0,4},{1,5},{4,8},{5,9},{8,12},{9,13},{12,14},{13,15},{14,10},{15,... | collective-permute-start | bytes 405512 | tf_op jit(solution)/shard_map/ppermute | solution.py:353
  26.0 2.4 %collective-permute-start.14 = (bf16[528,128]{1,0:T(8,128)(2,1)S(1)}, bf16[528,128]{1,0:T(8,128)(2,1)S(1)}, u32[]{:S(2)}, u32[]{:S(2)}) collective-permute-start(bf16[528,128]{1,0:T(8,128)(2,1)S(1)} %collective-permute-done.5.refs_6_), channel_id=1, source_target_pairs={{0,1},{1,0},{2,3},{3,2},{4,5},{5,4},{6,7},{7,6},{8,9},{9,8},{10,11... | collective-permute-start | bytes 405512 | tf_op jit(solution)/shard_map/ppermute | solution.py:353
where the time goes:
time: 31.1 us; the launch traced here: 30.9 us
  Pallas kernels  13.8 us (44%)
  starting transfers between devices  9.99 us (32%)
  waiting for transfers between devices  6.39 us (21%)
  between operations  0.75 us (2%)
    ppermute x15, starting transfers between devices, per_device(): send = lambda x, pairs: lax.ppermute(x, 'loop', pairs)  9.99 us
    ppermute x15, waiting for transfers between devices, per_device(): send = lambda x, pairs: lax.ppermute(x, 'loop', pairs)  6.39 us
    pallas_call x3, Pallas kernels, local(): pl.pallas_call(functools.partial(local_kernel, first=first, count=count,...  6.18 us
    pallas_call x2, Pallas kernels, partial(): pl.pallas_call(functools.partial(partial_kernel, have=have, spans=spans,...  4.24 us
    pallas_call x1, Pallas kernels, per_device(): pl.pallas_call(functools.partial(final_kernel, spans=groups, batch=-(-req...  2.43 us
    pallas_call x1, Pallas kernels, per_device(): pl.pallas_call(functools.partial(pack_kernel, heads=heads, block=block),...  0.91 us
  transfers between devices with their start and end apart: 15, of which 5 were waited for; matrix products, arithmetic and copies ran while one was open for 0% of the time, Pallas kernels for 34%

commit v1 on v0

--- a/solution.py
+++ b/solution.py
@@ -125,7 +125,7 @@
             kv[place[0], pl.ds(place[1], ref.shape[0]), :] = ref[...]
     for p in range(blocks):
         tag = kv[p, pl.ds(2 * heads * block, ID_ROWS), :].astype(jnp.float32)
-        slot_of[jnp.max(tag[:half] * 256.0 + tag[half:]).astype(jnp.int32)] = p
+        slot_of[(tag[:half] * 256.0 + tag[half:]).astype(jnp.int32)[0, 0]] = p
     for r in range(requests):
         places = [slot_of[list_ref[j, r]] for j in range(named)]
         (near_out, near_top, near_sum), i = home[r]
@@ -162,11 +162,11 @@
 
 
 def partial_kernel(
-    list_ref, q_ref, *refs, have, spans, collect, heads, block, named, steps, group, factor,
+    list_ref, q_ref, *refs, have, first, home, collect, heads, block, named, steps, group, factor,
 ):
-    pieces = len(spans)
+    pieces = 1 + max(p for p, _ in home)
     parts, refs = refs[: 3 * pieces], refs[3 * pieces :]
-    home = [(parts[3 * p : 3 * p + 3], i) for p, (_, count) in enumerate(spans) for i in range(count)]
+    home = [(parts[3 * p : 3 * p + 3], i) for p, i in home]
     if collect:
         loads, (kv, out_ref, top_ref, sum_ref, slot_of) = refs[:have], refs[have:]
         for p in range(have):
@@ -179,10 +179,10 @@
         slot_of[p] = -1
     for p in range(have):
         tag = kv[p, pl.ds(2 * heads * block, ID_ROWS), :].astype(jnp.float32)
-        slot_of[jnp.max(tag[:half] * 256.0 + tag[half:]).astype(jnp.int32)] = p
+        slot_of[(tag[:half] * 256.0 + tag[half:]).astype(jnp.int32)[0, 0]] = p
     which = lax.broadcasted_iota(jnp.int32, (1, named * block), 1) // block
     for o, ((near_out, near_top, near_sum), i) in enumerate(home):
-        r = spans[0][0] + o
+        r = first + o
         spots = [slot_of[list_ref[j, r]] for j in range(named)]
         places = [jnp.maximum(x, 0) for x in spots]
         bias = jnp.zeros(which.shape, jnp.float32)
@@ -224,7 +224,7 @@
     numbers = []
     for load in loads:
         tag = load[pl.ds(2 * heads * block, ID_ROWS), :].astype(jnp.float32)
-        numbers.append(jnp.max(tag[:half] * 256.0 + tag[half:]).astype(jnp.int32))
+        numbers.append((tag[:half] * 256.0 + tag[half:]).astype(jnp.int32)[0, 0])
     which = lax.broadcasted_iota(jnp.int32, (1, 2 * block), 1) // block
     outs = []
     for start in range(0, len(home), batch):
@@ -389,28 +389,36 @@
             parts += local(piece, suffix_len, held)
         sizes = dict(heads=heads, block=block, named=named, steps=steps, group=group, factor=factor)
 
-        def partial(spans, parts, lists, sources, collect):
-            count = sum(n for _, n in spans)
+        where = [(p, i) for p, (_, n) in enumerate(spans) for i in range(n)]
+
+        def partial(first, count, lists, sources, collect):
+            home = where[first : first + count]
+            low = home[0][0]
+            near_parts = parts[3 * low : 3 * home[-1][0] + 3]
+            home = [(p - low, i) for p, i in home]
             have = devices - 2
             stats = [pltpu.VMEM((count, heads, rows, width), jnp.float32)] * 3
             made = [pltpu.VMEM((have, load_rows, width), kind)] if collect else []
             return pl.pallas_call(
-                functools.partial(partial_kernel, have=have, spans=spans, collect=collect, **sizes),
+                functools.partial(
+                    partial_kernel, have=have, first=first, home=home, collect=collect, **sizes
+                ),
                 out_shape=made + stats,
-                in_specs=[smem] + [vmem] * (1 + len(parts) + len(sources)),
+                in_specs=[smem] + [vmem] * (1 + len(near_parts) + len(sources)),
                 out_specs=[vmem] * len(made + stats),
                 scratch_shapes=[pltpu.SMEM((devices,), jnp.int32)],
                 compiler_params=limit(4),
-            )(lists, *[near(x) for x in (held[0], *parts, *sources)])
-
-        collected, *early = partial(spans[:1], parts[:3], lists, loads, True)
+            )(lists, *[near(x) for x in (held[0], *near_parts, *sources)])
+
+        split = requests // 2
+        collected, *early = partial(0, split, lists, loads, True)
         right, *early = tie(right, *early)
         lists, right = tie(lists, right)
         other = send(right, swap)
-        late = partial(spans[1:], parts[3:], lists, [collected], False)
-        groups = [spans[0], (spans[1][0], requests - spans[1][0])]
+        late = partial(split, requests - split, lists, [collected], False)
+        groups = [(0, split), (split, requests - split)]
         return pl.pallas_call(
-            functools.partial(final_kernel, spans=groups, batch=-(-requests // 2), **sizes),
+            functools.partial(final_kernel, spans=groups, batch=requests, **sizes),
             out_shape=jax.ShapeDtypeStruct(queries.shape, kind),
             in_specs=[smem] + [vmem] * 9,
             out_specs=far,

time: 31.1 us -> 32.2 us (1.035)
  waiting for transfers between devices: 6.39 us -> 7.61 us
    ppermute x15, waiting for transfers between devices: 6.39 us -> 7.61 us  [per_device(): send = lambda x, pairs: lax.ppermute(x, 'loop', pairs)]
  transfers between devices with their start and end apart: 15 -> 15, of which waited for: 5 -> 5; matrix products, arithmetic and copies ran while one was open for 0% -> 0% of each run, Pallas kernels for 34% -> 32%
where the time goes in v1:
time: 32.2 us; the launch traced here: 32 us
  Pallas kernels  13.6 us (42%)
  starting transfers between devices  9.96 us (31%)
  waiting for transfers between devices  7.61 us (24%)
  between operations  0.75 us (2%)
    ppermute x15, starting transfers between devices, per_device(): send = lambda x, pairs: lax.ppermute(x, 'loop', pairs)  9.96 us
    ppermute x15, waiting for transfers between devices, per_device(): send = lambda x, pairs: lax.ppermute(x, 'loop', pairs)  7.61 us
    pallas_call x3, Pallas kernels, local(): pl.pallas_call(functools.partial(local_kernel, first=first, count=count,...  6.18 us
    pallas_call x2, Pallas kernels, partial(): pl.pallas_call(functools.partial(partial_kernel, have=have, first=first,...  4.11 us
    pallas_call x1, Pallas kernels, per_device(): pl.pallas_call(functools.partial(final_kernel, spans=groups, batch=reques...  2.45 us
    pallas_call x1, Pallas kernels, per_device(): pl.pallas_call(functools.partial(pack_kernel, heads=heads, block=block),...  0.91 us
  transfers between devices with their start and end apart: 15, of which 5 were waited for; matrix products, arithmetic and copies ran while one was open for 0% of the time, Pallas kernels for 32%

profile of v1, /device:TPU:0, one launch (start us, length us, event | category | flops | bytes accessed | tf_op | source)
XLA Modules:
  0.0 32.0 jit_solution(11583310234597477050)
XLA Ops:
  0.7 0.9 %pack.1.refs_6_ = bf16[528,128]{1,0:T(8,128)(2,1)S(1)} custom-call(s32[1]{0:T(128)S(6)} %copy.11.id_ref, bf16[256,128]{1,0:T(8,128)(2,1)} %bitcast.12, bf16[256,128]{1,0:T(8,128)(2,1)} %bitcast.13), custom_call_target="tpu_custom_call" | custom-call | tf_op jit(solution)/shard_map/pack/pallas_call | solution.py:296
  1.6 0.0 copy-start.1
  1.6 3.1 %collective-permute-start = (bf16[528,128]{1,0:T(8,128)(2,1)S(1)}, bf16[528,128]{1,0:T(8,128)(2,1)S(1)}, u32[]{:S(2)}, u32[]{:S(2)}) collective-permute-start(bf16[528,128]{1,0:T(8,128)(2,1)S(1)} %pack.1.refs_6_), channel_id=1, source_target_pairs={{0,4},{1,5},{4,8},{5,9},{8,12},{9,13},{12,14},{13,15},{14,10},{15,... | collective-permute-start | bytes 405512 | tf_op jit(solution)/shard_map/ppermute | solution.py:353
  4.7 0.0 collective-permute-start.2
  4.7 3.1 %shard_map.100 = (bf16[8,4,64,128]{3,2,1,0:T(8,128)(2,1)S(1)}, bf16[8,16,128]{2,1,0:T(8,128)(2,1)S(1)}, bf16[8,16,128]{2,1,0:T(8,128)(2,1)S(1)}, bf16[8,1024,128...) custom-call(s32[8]{0:T(128)} %len_ref.3, ...), custom_call_target="tpu_custom_call" | custom-call | tf_op jit(solution)/shard_map/pallas_call | solution.py:329
  7.8 0.5 %collective-permute-done.refs_7_ = bf16[528,128]{1,0:T(8,128)(2,1)S(1)} collective-permute-done((bf16[528,128]{1,0:T(8,128)(2,1)S(1)}, bf16[528,128]{1,0:T(8,128)(2,1)S(1)}, u32[]{:S(2)}, u32[]{:S(2)}) %collective-permute-start) | collective-permute-done | bytes 135200 | tf_op jit(solution)/shard_map/ppermute | solution.py:353
  8.2 1.8 %collective-permute-start.1 = (bf16[528,128]{1,0:T(8,128)(2,1)S(1)}, bf16[528,128]{1,0:T(8,128)(2,1)S(1)}, u32[]{:S(2)}, u32[]{:S(2)}) collective-permute-start(bf16[528,128]{1,0:T(8,128)(2,1)S(1)} %collective-permute-done.refs_7_), channel_id=1, source_target_pairs={{0,4},{1,5},{4,8},{5,9},{8,12},{9,13},{12,14},{13,15},{14,10},{15,... | collective-permute-start | bytes 405512 | tf_op jit(solution)/shard_map/ppermute | solution.py:353
  10.0 0.0 collective-permute-done.2.refs_8_
  10.0 0.2 collective-permute-start.4
  10.2 0.0 collective-permute-start.7
  10.2 1.7 %shard_map.101 = (f32[3,4,64,128]{3,2,1,0:T(8,128)S(1)}, f32[3,4,64,128]{3,2,1,0:T(8,128)S(1)}, f32[3,4,64,128]{3,2,1,0:T(8,128)S(1)}) custom-call(s32[8]{0:T(128)S(1)} %copy-done.1, bf16[8,4,64,128]{3,2,1,0:T(8,128)(2,1)S(1)} %get-tuple-element.75.refs_0_.q_ref, bf16[8,16,128]{2,1,0:T(8,128)(2,1)S(1)} %get-tuple-element.76.refs_1_, ...), custom_call_target="tpu_custom_call" | custom-call | tf_op jit(solution)/shard_map/pallas_call | solution.py:329
  12.0 0.6 %collective-permute-start.8 = (bf16[528,128]{1,0:T(8,128)(2,1)S(1)}, bf16[528,128]{1,0:T(8,128)(2,1)S(1)}, u32[]{:S(2)}, u32[]{:S(2)}) collective-permute-start(bf16[528,128]{1,0:T(8,128)(2,1)S(1)} %collective-permute-done.refs_7_), channel_id=1, source_target_pairs={{0,1},{1,0},{2,3},{3,2},{4,5},{5,4},{6,7},{7,6},{8,9},{9,8},{10,11... | collective-permute-start | bytes 405512 | tf_op jit(solution)/shard_map/ppermute | solution.py:353
  12.6 0.7 %collective-permute-done.1.refs_9_ = bf16[528,128]{1,0:T(8,128)(2,1)S(1)} collective-permute-done((bf16[528,128]{1,0:T(8,128)(2,1)S(1)}, bf16[528,128]{1,0:T(8,128)(2,1)S(1)}, u32[]{:S(2)}, u32[]{:S(2)}) %collective-permute-start.1) | collective-permute-done | bytes 135200 | tf_op jit(solution)/shard_map/ppermute | solution.py:353
  13.2 1.8 %collective-permute-start.3 = (bf16[528,128]{1,0:T(8,128)(2,1)S(1)}, bf16[528,128]{1,0:T(8,128)(2,1)S(1)}, u32[]{:S(2)}, u32[]{:S(2)}) collective-permute-start(bf16[528,128]{1,0:T(8,128)(2,1)S(1)} %collective-permute-done.1.refs_9_), channel_id=1, source_target_pairs={{0,4},{1,5},{4,8},{5,9},{8,12},{9,13},{12,14},{13,15},{14,10},{15,... | collective-permute-start | bytes 405512 | tf_op jit(solution)/shard_map/ppermute | solution.py:353
  15.0 0.2 collective-permute-start.6
  15.3 0.0 collective-permute-done.7.refs_13_
  15.3 0.5 %collective-permute-start.10 = (bf16[528,128]{1,0:T(8,128)(2,1)S(1)}, bf16[528,128]{1,0:T(8,128)(2,1)S(1)}, u32[]{:S(2)}, u32[]{:S(2)}) collective-permute-start(bf16[528,128]{1,0:T(8,128)(2,1)S(1)} %collective-permute-done.1.refs_9_), channel_id=1, source_target_pairs={{0,1},{1,0},{2,3},{3,2},{4,5},{5,4},{6,7},{7,6},{8,9},{9,8},{10,11... | collective-permute-start | bytes 405512 | tf_op jit(solution)/shard_map/ppermute | solution.py:353
  15.8 0.0 collective-permute-done.8.refs_14_
  15.8 0.1 collective-permute-start.11
  15.8 2.4 %collective-permute-done.3.refs_11_ = bf16[528,128]{1,0:T(8,128)(2,1)S(1)} collective-permute-done((bf16[528,128]{1,0:T(8,128)(2,1)S(1)}, bf16[528,128]{1,0:T(8,128)(2,1)S(1)}, u32[]{:S(2)}, u32[]{:S(2)}) %collective-permute-start.3) | collective-permute-done | bytes 135200 | tf_op jit(solution)/shard_map/ppermute | solution.py:353
  18.2 1.8 %collective-permute-done.6.refs_12_ = bf16[528,128]{1,0:T(8,128)(2,1)S(1)} collective-permute-done((bf16[528,128]{1,0:T(8,128)(2,1)S(1)}, bf16[528,128]{1,0:T(8,128)(2,1)S(1)}, u32[]{:S(2)}, u32[]{:S(2)}) %collective-permute-start.6) | collective-permute-done | bytes 135200 | tf_op jit(solution)/shard_map/ppermute | solution.py:353
  20.0 0.0 collective-permute-start.13
  20.0 1.4 %shard_map.102 = (f32[2,4,64,128]{3,2,1,0:T(8,128)S(1)}, f32[2,4,64,128]{3,2,1,0:T(8,128)S(1)}, f32[2,4,64,128]{3,2,1,0:T(8,128)S(1)}) custom-call(s32[8]{0:T(128)S(1)} %copy-done.1, bf16[8,4,64,128]{3,2,1,0:T(8,128)(2,1)S(1)} %get-tuple-element.75.refs_0_.q_ref, bf16[8,16,128]{2,1,0:T(8,128)(2,1)S(1)} %get-tuple-element.76.refs_1_, ...), custom_call_target="tpu_custom_call" | custom-call | tf_op jit(solution)/shard_map/pallas_call | solution.py:329
  21.4 1.6 %collective-permute-start.5 = (bf16[528,128]{1,0:T(8,128)(2,1)S(1)}, bf16[528,128]{1,0:T(8,128)(2,1)S(1)}, u32[]{:S(2)}, u32[]{:S(2)}) collective-permute-start(bf16[528,128]{1,0:T(8,128)(2,1)S(1)} %collective-permute-done.3.refs_11_), channel_id=1, source_target_pairs={{0,4},{1,5},{4,8},{5,9},{8,12},{9,13},{12,14},{13,15},{14,10},{15,... | collective-permute-start | bytes 405512 | tf_op jit(solution)/shard_map/ppermute | solution.py:353
  23.1 0.0 collective-permute-done.10.refs_16_
  23.1 0.0 collective-permute-done.11.refs_17_
  23.1 0.0 collective-permute-done.12.refs_18_
  23.1 0.0 collective-permute-done.13.refs_19_
  23.1 2.1 %shard_map.103 = (bf16[14,528,128]{2,1,0:T(8,128)(2,1)S(1)}, f32[4,4,64,128]{3,2,1,0:T(8,128)S(1)}, f32[4,4,64,128]{3,2,1,0:T(8,128)S(1)}, f32[4,4,64,128]{3,2,1,0:T(8,128)S(1)}) custom-call(s32[4,8]{1,0:T(4,128)S(1)} %bitcast.7, bf16[8,4,64,128]{3,2,1,0:T(8,128)(2,1)S(1)} %get-tuple-element.75.refs_0_.q_ref, ...), custom_call_target="tpu_custom_call" | custom-call | tf_op jit(solution)/shard_map/pallas_call | solution.py:402
  25.2 2.3 %collective-permute-done.5.refs_6_ = bf16[528,128]{1,0:T(8,128)(2,1)S(1)} collective-permute-done((bf16[528,128]{1,0:T(8,128)(2,1)S(1)}, bf16[528,128]{1,0:T(8,128)(2,1)S(1)}, u32[]{:S(2)}, u32[]{:S(2)}) %collective-permute-start.5) | collective-permute-done | bytes 135200 | tf_op jit(solution)/shard_map/ppermute | solution.py:353
  27.5 2.0 %shard_map.104 = (f32[4,4,64,128]{3,2,1,0:T(8,128)S(1)}, f32[4,4,64,128]{3,2,1,0:T(8,128)S(1)}, f32[4,4,64,128]{3,2,1,0:T(8,128)S(1)}) custom-call(s32[4,8]{1,0:T(4,128)S(1)} %bitcast.8, bf16[8,4,64,128]{3,2,1,0:T(8,128)(2,1)S(1)} %get-tuple-element.75.refs_0_.q_ref, f32[3,4,64,128]{3,2,1,0:T(8,128)S(1)} %get-tuple-element.93.refs_3_.refs_0_, ...), custom_call_target="tpu_custom_call" | custom-call | tf_op jit(solution)/shard_map/pallas_call | solution.py:402
  29.5 2.5 %final.1 = bf16[8,4,64,128]{3,2,1,0:T(8,128)(2,1)} custom-call(s32[4,8]{1,0:T(4,128)S(1)} %bitcast.9, bf16[8,4,64,128]{3,2,1,0:T(8,128)(2,1)S(1)} %get-tuple-element.75.refs_0_.q_ref, f32[4,4,64,128]{3,2,1,0:T(8,128)S(1)} %get-tuple-element.102.refs_0_, f32[4,4,64,128]{3,2,1,0:T(8,128)S(1)} %get-tuple-element.103.refs_1_, ...), custom_call_target="tpu_custom_call" | custom-call | tf_op jit(solution)/shard_map/final/pallas_call | solution.py:420
  (9 shorter events, 0.0 us)
Async XLA Ops:
  1.6 8.7 %copy-start.1 = (s32[8]{0:T(128)S(1)}, s32[8]{0:T(128)}, u32[]{:S(2)}) copy-start(s32[8]{0:T(128)} %len_ref.3) | copy-start | bytes 100
  1.6 6.6 %collective-permute-start = (bf16[528,128]{1,0:T(8,128)(2,1)S(1)}, bf16[528,128]{1,0:T(8,128)(2,1)S(1)}, u32[]{:S(2)}, u32[]{:S(2)}) collective-permute-start(bf16[528,128]{1,0:T(8,128)(2,1)S(1)} %pack.1.refs_6_), channel_id=1, source_target_pairs={{0,4},{1,5},{4,8},{5,9},{8,12},{9,13},{12,14},{13,15},{14,10},{15,... | collective-permute-start | bytes 405512 | tf_op jit(solution)/shard_map/ppermute | solution.py:353
  4.7 5.3 %collective-permute-start.2 = (bf16[528,128]{1,0:T(8,128)(2,1)S(1)}, bf16[528,128]{1,0:T(8,128)(2,1)S(1)}, u32[]{:S(2)}, u32[]{:S(2)}) collective-permute-start(bf16[528,128]{1,0:T(8,128)(2,1)S(1)} %pack.1.refs_6_), channel_id=1, source_target_pairs={{4,0},{5,1},{8,4},{9,5},{12,8},{13,9},{14,12},{15,13},{10,14},{11,... | collective-permute-start | bytes 405512 | tf_op jit(solution)/shard_map/ppermute | solution.py:353
  8.2 5.0 %collective-permute-start.1 = (bf16[528,128]{1,0:T(8,128)(2,1)S(1)}, bf16[528,128]{1,0:T(8,128)(2,1)S(1)}, u32[]{:S(2)}, u32[]{:S(2)}) collective-permute-start(bf16[528,128]{1,0:T(8,128)(2,1)S(1)} %collective-permute-done.refs_7_), channel_id=1, source_target_pairs={{0,4},{1,5},{4,8},{5,9},{8,12},{9,13},{12,14},{13,15},{14,10},{15,... | collective-permute-start | bytes 405512 | tf_op jit(solution)/shard_map/ppermute | solution.py:353
  10.0 5.0 %collective-permute-start.4 = (bf16[528,128]{1,0:T(8,128)(2,1)S(1)}, bf16[528,128]{1,0:T(8,128)(2,1)S(1)}, u32[]{:S(2)}, u32[]{:S(2)}) collective-permute-start(bf16[528,128]{1,0:T(8,128)(2,1)S(1)} %collective-permute-done.2.refs_8_), channel_id=1, source_target_pairs={{4,0},{5,1},{8,4},{9,5},{12,8},{13,9},{14,12},{15,13},{10,14},{11,... | collective-permute-start | bytes 405512 | tf_op jit(solution)/shard_map/ppermute | solution.py:353
  10.2 5.0 %collective-permute-start.7 = (bf16[528,128]{1,0:T(8,128)(2,1)S(1)}, bf16[528,128]{1,0:T(8,128)(2,1)S(1)}, u32[]{:S(2)}, u32[]{:S(2)}) collective-permute-start(bf16[528,128]{1,0:T(8,128)(2,1)S(1)} %pack.1.refs_6_), channel_id=1, source_target_pairs={{0,1},{1,0},{2,3},{3,2},{4,5},{5,4},{6,7},{7,6},{8,9},{9,8},{10,11... | collective-permute-start | bytes 405512 | tf_op jit(solution)/shard_map/ppermute | solution.py:353
  12.0 3.8 %collective-permute-start.8 = (bf16[528,128]{1,0:T(8,128)(2,1)S(1)}, bf16[528,128]{1,0:T(8,128)(2,1)S(1)}, u32[]{:S(2)}, u32[]{:S(2)}) collective-permute-start(bf16[528,128]{1,0:T(8,128)(2,1)S(1)} %collective-permute-done.refs_7_), channel_id=1, source_target_pairs={{0,1},{1,0},{2,3},{3,2},{4,5},{5,4},{6,7},{7,6},{8,9},{9,8},{10,11... | collective-permute-start | bytes 405512 | tf_op jit(solution)/shard_map/ppermute | solution.py:353
  13.2 9.9 %copy-start = (s32[8,4]{0,1:T(4,128)S(1)}, s32[8,4]{0,1:T(4,128)}, u32[]{:S(2)}) copy-start(s32[8,4]{0,1:T(4,128)} %param.19) | copy-start | bytes 388
  13.2 5.0 %collective-permute-start.3 = (bf16[528,128]{1,0:T(8,128)(2,1)S(1)}, bf16[528,128]{1,0:T(8,128)(2,1)S(1)}, u32[]{:S(2)}, u32[]{:S(2)}) collective-permute-start(bf16[528,128]{1,0:T(8,128)(2,1)S(1)} %collective-permute-done.1.refs_9_), channel_id=1, source_target_pairs={{0,4},{1,5},{4,8},{5,9},{8,12},{9,13},{12,14},{13,15},{14,10},{15,... | collective-permute-start | bytes 405512 | tf_op jit(solution)/shard_map/ppermute | solution.py:353
  15.0 5.0 %collective-permute-start.6 = (bf16[528,128]{1,0:T(8,128)(2,1)S(1)}, bf16[528,128]{1,0:T(8,128)(2,1)S(1)}, u32[]{:S(2)}, u32[]{:S(2)}) collective-permute-start(bf16[528,128]{1,0:T(8,128)(2,1)S(1)} %collective-permute-done.4.refs_10_), channel_id=1, source_target_pairs={{4,0},{5,1},{8,4},{9,5},{12,8},{13,9},{14,12},{15,13},{10,14},{11,... | collective-permute-start | bytes 405512 | tf_op jit(solution)/shard_map/ppermute | solution.py:353
  15.3 6.2 %collective-permute-start.9 = (bf16[528,128]{1,0:T(8,128)(2,1)S(1)}, bf16[528,128]{1,0:T(8,128)(2,1)S(1)}, u32[]{:S(2)}, u32[]{:S(2)}) collective-permute-start(bf16[528,128]{1,0:T(8,128)(2,1)S(1)} %collective-permute-done.2.refs_8_), channel_id=1, source_target_pairs={{0,1},{1,0},{2,3},{3,2},{4,5},{5,4},{6,7},{7,6},{8,9},{9,8},{10,11... | collective-permute-start | bytes 405512 | tf_op jit(solution)/shard_map/ppermute | solution.py:353
  15.3 7.8 %collective-permute-start.10 = (bf16[528,128]{1,0:T(8,128)(2,1)S(1)}, bf16[528,128]{1,0:T(8,128)(2,1)S(1)}, u32[]{:S(2)}, u32[]{:S(2)}) collective-permute-start(bf16[528,128]{1,0:T(8,128)(2,1)S(1)} %collective-permute-done.1.refs_9_), channel_id=1, source_target_pairs={{0,1},{1,0},{2,3},{3,2},{4,5},{5,4},{6,7},{7,6},{8,9},{9,8},{10,11... | collective-permute-start | bytes 405512 | tf_op jit(solution)/shard_map/ppermute | solution.py:353
  15.8 7.3 %collective-permute-start.11 = (bf16[528,128]{1,0:T(8,128)(2,1)S(1)}, bf16[528,128]{1,0:T(8,128)(2,1)S(1)}, u32[]{:S(2)}, u32[]{:S(2)}) collective-permute-start(bf16[528,128]{1,0:T(8,128)(2,1)S(1)} %collective-permute-done.4.refs_10_), channel_id=1, source_target_pairs={{0,1},{1,0},{2,3},{3,2},{4,5},{5,4},{6,7},{7,6},{8,9},{9,8},{10,11... | collective-permute-start | bytes 405512 | tf_op jit(solution)/shard_map/ppermute | solution.py:353
  18.2 4.8 %collective-permute-start.12 = (bf16[528,128]{1,0:T(8,128)(2,1)S(1)}, bf16[528,128]{1,0:T(8,128)(2,1)S(1)}, u32[]{:S(2)}, u32[]{:S(2)}) collective-permute-start(bf16[528,128]{1,0:T(8,128)(2,1)S(1)} %collective-permute-done.3.refs_11_), channel_id=1, source_target_pairs={{0,1},{1,0},{2,3},{3,2},{4,5},{5,4},{6,7},{7,6},{8,9},{9,8},{10,11... | collective-permute-start | bytes 405512 | tf_op jit(solution)/shard_map/ppermute | solution.py:353
  20.0 3.1 %collective-permute-start.13 = (bf16[528,128]{1,0:T(8,128)(2,1)S(1)}, bf16[528,128]{1,0:T(8,128)(2,1)S(1)}, u32[]{:S(2)}, u32[]{:S(2)}) collective-permute-start(bf16[528,128]{1,0:T(8,128)(2,1)S(1)} %collective-permute-done.6.refs_12_), channel_id=1, source_target_pairs={{0,1},{1,0},{2,3},{3,2},{4,5},{5,4},{6,7},{7,6},{8,9},{9,8},{10,11... | collective-permute-start | bytes 405512 | tf_op jit(solution)/shard_map/ppermute | solution.py:353
  21.4 6.0 %collective-permute-start.5 = (bf16[528,128]{1,0:T(8,128)(2,1)S(1)}, bf16[528,128]{1,0:T(8,128)(2,1)S(1)}, u32[]{:S(2)}, u32[]{:S(2)}) collective-permute-start(bf16[528,128]{1,0:T(8,128)(2,1)S(1)} %collective-permute-done.3.refs_11_), channel_id=1, source_target_pairs={{0,4},{1,5},{4,8},{5,9},{8,12},{9,13},{12,14},{13,15},{14,10},{15,... | collective-permute-start | bytes 405512 | tf_op jit(solution)/shard_map/ppermute | solution.py:353
  27.5 2.0 %collective-permute-start.14 = (bf16[528,128]{1,0:T(8,128)(2,1)S(1)}, bf16[528,128]{1,0:T(8,128)(2,1)S(1)}, u32[]{:S(2)}, u32[]{:S(2)}) collective-permute-start(bf16[528,128]{1,0:T(8,128)(2,1)S(1)} %collective-permute-done.5.refs_6_), channel_id=1, source_target_pairs={{0,1},{1,0},{2,3},{3,2},{4,5},{5,4},{6,7},{7,6},{8,9},{9,8},{10,11... | collective-permute-start | bytes 405512 | tf_op jit(solution)/shard_map/ppermute | solution.py:353
